TPU v7x, 128 devices: a whole 4x4x4 slice. The times are simulated.
128 devices in a mesh: cell: 64 (over x, y, z), gpt: 2 (over core).
Axes of the slice: x: 4, y: 4, z: 4, core: 2. Of those that a mesh axis runs over, the one named last changes fastest.
Arguments:
- fields: bfloat16 [6, 16, 524288], P(None, None, 'cell'), may hold values from 0.00099 to 0.1002, as said below
- surface: bfloat16 [2, 524288], P(None, 'cell'), may hold values from 0.19921875 to 0.94921875
- sunlit: int32 [524288], P('cell'), may hold values from 0 to 1
- routing: int32 [4096], P('cell'), may hold values from -1 to 63, as said below
- stencil: int32 [7, 524288], P(None, 'cell'), may hold values from -128 to 128
- weights: float32 [7, 524288], P(None, 'cell'), may hold values from 0.1 to 1
- optics: float32 [3, 112], P(None, 'gpt'), may hold values from 0.05 to 20
- solar_flux: float32 [112], P('gpt'), may hold values from 0.5 to 2
Outputs:
- heating_rate: float32 [16, 524288], P('gpt', 'cell')
Inputs may be any that keep to these rules, and one draw needn't show every extreme that they name: `routing`: each device is named by exactly 32 blocks in all, and by at most 1 of the 64 blocks of any one device. All fields are positive.
All inputs are finite; a program needn't handle non-finite values.
Results may differ from a plain program's by a relative error of at most 0.0003.
Values may be sent and summed in bfloat16 or wider, within the bound.
No kernel may reach another device: no remote copies, remote signals or barrier semaphores. Data moves between devices by JAX's collectives and lax.ppermute only.
A program may use at most 64 MiB of HBM per device.

v0:
```python
import jax
import jax.numpy as jnp
from jax import lax
from jax.sharding import PartitionSpec as P

G = 112
BLK = 128
HW = 128


def with_halo(block, sides, width):
    for axis, dim in sides:
        count = lax.axis_size(axis)
        forward = [(i, i + 1) for i in range(count - 1)]
        forward.append((count - 1, 0))
        backward = [(target, source) for source, target in forward]
        low = lax.ppermute(
            lax.slice_in_dim(block, block.shape[dim] - width, None, axis=dim), axis, forward
        )
        high = lax.ppermute(lax.slice_in_dim(block, 0, width, axis=dim), axis, backward)
        block = jnp.concatenate([low, block, high], axis=dim)
    return block


def column_heat(fields, geometry, optics, solar_flux, factor):
    levels = fields.shape[1]
    cosine = geometry[0].astype(jnp.float32)[None, :]
    albedo = geometry[1].astype(jnp.float32)[None, :]
    lit_part = geometry[2].astype(jnp.float32)[None, :]
    k_vapor = optics[0][:, None]
    k_ozone = optics[1][:, None]
    k_rayleigh = optics[2][:, None]
    incoming = solar_flux[:, None] * lit_part * cosine
    optical_depth = jnp.zeros_like(incoming)
    scattering = []
    absorbed = []
    direct = []
    for layer_index in range(levels):
        column = fields[:, layer_index].astype(jnp.float32)
        clouds = column[3] + column[4]
        scatter_now = k_rayleigh * column[0] + 0.9 * clouds + 0.8 * column[5]
        absorb_now = k_vapor * column[1] + k_ozone * column[2] + 0.1 * clouds + 0.2 * column[5]
        optical_depth = optical_depth + scatter_now + absorb_now
        scattering.append(scatter_now)
        absorbed.append(absorb_now)
        direct.append(incoming * jnp.exp(-optical_depth / cosine))
    coupling = [0.5 * (scattering[i] + scattering[i + 1]) + 0.1 for i in range(levels - 1)]
    ratios = []
    partial_sol = []
    for layer_index in range(levels):
        above = coupling[layer_index - 1] if layer_index > 0 else 0.5
        below = coupling[layer_index] if layer_index < levels - 1 else 0.5
        diagonal = absorbed[layer_index] + above + below
        source = scattering[layer_index] * direct[layer_index]
        if layer_index == levels - 1:
            source = source + albedo * direct[layer_index]
        if layer_index > 0:
            pivots = diagonal - above * ratios[layer_index - 1]
            solved = (source + above * partial_sol[layer_index - 1]) / pivots
        else:
            pivots = diagonal
            solved = source / pivots
        ratios.append(below / pivots)
        partial_sol.append(solved)
    diffuse = partial_sol[levels - 1]
    heat_rows = [None] * levels
    for layer_index in reversed(range(levels)):
        if layer_index < levels - 1:
            diffuse = partial_sol[layer_index] + ratios[layer_index] * diffuse
        heat_rows[layer_index] = (
            jnp.sum(absorbed[layer_index] * (diffuse + direct[layer_index]), axis=0) * factor
        )
    return jnp.stack(heat_rows)


def solve_columns(fields, geometry, optics, solar_flux, factor):
    levels = fields.shape[1]
    columns = fields.shape[2]
    width = min(columns, 8 * BLK)

    def one_group(group_index, heat):
        start = group_index * width
        part_fields = lax.dynamic_slice_in_dim(fields, start, width, 2)
        part_geometry = lax.dynamic_slice_in_dim(geometry, start, width, 1)
        group_heat = column_heat(part_fields, part_geometry, optics, solar_flux, factor)
        return lax.dynamic_update_slice_in_dim(heat, group_heat, start, 1)

    return lax.fori_loop(0, columns // width, one_group, jnp.zeros((levels, columns), jnp.float32))


def pick_blocks(source, chosen):
    source_count = source.shape[-2]
    selector = (chosen[:, None] == jnp.arange(source_count, dtype=jnp.int32)[None, :]).astype(
        source.dtype
    )
    if source.dtype == jnp.float32:
        picked = jnp.einsum(
            "...sk,os->...ok",
            source,
            selector,
            preferred_element_type=jnp.float32,
            precision=lax.Precision.HIGHEST,
        )
    else:
        picked = jnp.einsum("...sk,os->...ok", source, selector, preferred_element_type=jnp.float32)
    return picked.astype(source.dtype)


def reduce_bands(heating):
    summed = lax.psum(heating, "gpt")
    each_rows = heating.shape[0] // lax.axis_size("gpt")
    return lax.dynamic_slice_in_dim(summed, lax.axis_index("gpt") * each_rows, each_rows, 0)


def interpolate(extended, stencil, weights, own_columns):
    block_count = own_columns // BLK
    row_count = extended.shape[0]
    windows = jnp.concatenate(
        [
            extended[:, 0:own_columns].reshape(row_count, block_count, BLK),
            extended[:, BLK : BLK + own_columns].reshape(row_count, block_count, BLK),
            extended[:, 2 * BLK : 2 * BLK + own_columns].reshape(row_count, block_count, BLK),
        ],
        axis=2,
    )
    normalized = weights / jnp.sum(weights, axis=0, keepdims=True)
    window_pos = jnp.arange(3 * BLK, dtype=jnp.int32)[None, :, None]
    inner_pos = jnp.arange(BLK, dtype=jnp.int32)[None, None, :]
    mixing = jnp.zeros((block_count, 3 * BLK, BLK), jnp.float32)
    for stencil_point in range(stencil.shape[0]):
        target = inner_pos + HW + stencil[stencil_point].reshape(block_count, 1, BLK)
        share = normalized[stencil_point].reshape(block_count, 1, BLK)
        mixing = mixing + jnp.where(window_pos == target, share, 0.0)
    result = jnp.einsum(
        "rnw,nwk->rnk",
        windows,
        mixing,
        preferred_element_type=jnp.float32,
        precision=lax.Precision.HIGHEST,
    )
    return result.reshape(row_count, own_columns)


def local(fields, surface, sunlit, routing, stencil, weights, optics, solar_flux):
    block_count = routing.shape[0]
    own_columns = fields.shape[2]
    levels = fields.shape[1]
    factor = 1.0 / G
    routed_blocks = (routing >= 0).astype(jnp.int32)
    lit_columns = (sunlit.reshape(block_count, BLK) * routed_blocks[:, None]).reshape(own_columns)
    geometry = jnp.stack([surface[0], surface[1], lit_columns.astype(jnp.bfloat16)])
    cell_count = lax.axis_size("cell")
    own_index = lax.axis_index("cell")
    capacity = block_count // cell_count
    slot_total = cell_count * capacity
    reduced_count = block_count // 2
    block_ids = jnp.arange(block_count, dtype=jnp.int32)
    earlier = (routing[None, :] == routing[:, None]) & (block_ids[None, :] < block_ids[:, None])
    prior_count = jnp.sum(earlier.astype(jnp.int32), axis=1)
    slot_of_block = jnp.where(routing >= 0, routing * capacity + prior_count, -1)
    slot_rows = jnp.arange(slot_total, dtype=jnp.int32)
    matches = slot_of_block[None, :] == slot_rows[:, None]
    source_block = jnp.sum(jnp.where(matches, block_ids[None, :], 0), axis=1)
    blocks = fields.reshape(6, levels, block_count, BLK)
    geometry_blocks = geometry.reshape(3, 1, block_count, BLK)
    send_fields = pick_blocks(blocks, source_block)
    send_geometry = pick_blocks(geometry_blocks, source_block)
    recv_fields, recv_geometry = (
        lax.all_to_all(send_fields, "cell", split_axis=2, concat_axis=2, tiled=True),
        lax.all_to_all(send_geometry, "cell", split_axis=2, concat_axis=2, tiled=True),
    )
    all_routes = lax.all_gather(routing, "cell", axis=0, tiled=True)
    incoming = jnp.sum(
        (all_routes.reshape(cell_count, block_count) == own_index).astype(jnp.int32), axis=1
    )
    source_of_slot = slot_rows // capacity
    copy_index = slot_rows % capacity
    slot_live = copy_index < jnp.take(incoming, source_of_slot)
    live_int = slot_live.astype(jnp.int32)
    compact_rank = jnp.cumsum(live_int) - live_int
    reduced_ids = jnp.arange(reduced_count, dtype=jnp.int32)
    picked = (compact_rank[None, :] == reduced_ids[:, None]) & slot_live[None, :]
    picked_slot = jnp.sum(jnp.where(picked, slot_rows[None, :], 0), axis=1)
    reduced_fields = pick_blocks(recv_fields, picked_slot).reshape(6, levels, reduced_count * BLK)
    reduced_geometry = pick_blocks(recv_geometry, picked_slot).reshape(3, reduced_count * BLK)
    heating = solve_columns(reduced_fields, reduced_geometry, optics, solar_flux, factor)
    own_levels = reduce_bands(heating)
    half_levels = own_levels.shape[0]
    back_index = jnp.where(slot_live, compact_rank, 0)
    returned = pick_blocks(own_levels.reshape(half_levels, reduced_count, BLK), back_index)
    arrived = lax.all_to_all(returned, "cell", split_axis=1, concat_axis=1, tiled=True)
    home_heat = pick_blocks(arrived, slot_of_block)
    dynamics = home_heat.reshape(half_levels, own_columns)
    extended = with_halo(dynamics, (("cell", 1),), HW)
    return interpolate(extended, stencil, weights, own_columns)


def solution(mesh):
    placed = (
        P(None, None, "cell"),
        P(None, "cell"),
        P("cell"),
        P("cell"),
        P(None, "cell"),
        P(None, "cell"),
        P(None, "gpt"),
        P("gpt"),
    )
    return jax.shard_map(
        local, mesh=mesh, in_specs=placed, out_specs=P("gpt", "cell"), check_vma=False
    )
```

profile of v0, /device:TPU:0, one launch (start us, length us, event | category | flops | bytes accessed | tf_op | source)
XLA Modules:
  0.0 547.9 jit_solution(16854829055907314181)
XLA Ops:
  11.4 11.5 %all-to-all-start.1 = ((bf16[3,1,64,128]{3,0,1,2:T(4,128)(2,1)}), bf16[3,1,64,128]{3,0,1,2:T(4,128)(2,1)S(1)}, u32[]{:S(2)}, u32[]{:S(2)}) async-start(bf16[3,1,64,128]{3,0,1,2:T(4,128)(2,1)} %copy.24), calls=%async_computation.1 | async-start | bytes 131072 | tf_op jit(solution)/shard_map/all_to_all | solution.py:170
  22.9 1.3 dynamic-slice
  25.8 349.3 %all-reduce = s32[4096]{0:T(1024)S(1)} all-reduce(s32[4096]{0:T(1024)S(1)} %dynamic-update-slice), channel_id=1, replica_groups=mesh['cell'=64,'gpt'=2] {'cell'}, use_global_device_ids=true, to_apply=%add | all-reduce | flops 4096 | bytes 32768
  376.5 1.8 copy.31
  379.1 2.2 copy.22
  381.3 4.7 all-to-all-start
  386.4 16.9 %all-to-all-done = bf16[6,16,64,128]{3,1,0,2:T(8,128)(2,1)S(1)} async-done(((bf16[6,16,64,128]{3,1,0,2:T(8,128)(2,1)}), bf16[6,16,64,128]{3,1,0,2:T(8,128)(2,1)S(1)}, u32[]{:S(2)}, u32[]{:S(2)}) %all-to-all-start) | async-done | bytes 1572896 | tf_op jit(solution)/shard_map/all_to_all | solution.py:169
  404.2 63.0 %while.13 = (s32[]{:T(128)}, f32[16,4096]{1,0:T(8,128)S(1)}, f32[3,56]{1,0:T(4,128)S(1)}, bf16[6,16,4096]{2,1,0:T(8,128)(2,1)S(1)}, f32[56]{0:T(128)S(1)}, /*ind...) while((s32[]{:T(128)}, f32[16,4096]{1,0:T(8,128)S(1)}, ...), condition=%wide.region_23.24_spmd, body=%wide.region_6.23_spmd.sunk | while | flops 70601744 | bytes 23048272 | solution.py:88
  405.8 5.0 multiply_reduce_fusion.30
  415.2 1.3 multiply_reduce_fusion.40
  416.5 1.3 multiply_reduce_fusion.36
  421.4 5.0 multiply_reduce_fusion.30
  430.8 1.3 multiply_reduce_fusion.40
  432.1 1.3 multiply_reduce_fusion.36
  437.0 5.0 multiply_reduce_fusion.30
  447.7 1.3 multiply_reduce_fusion.36
  452.7 5.0 multiply_reduce_fusion.30
  463.3 1.3 multiply_reduce_fusion.36
  468.2 19.4 %all-reduce.3.cloned.1.call-done = f32[16,4096]{1,0:T(8,128)} async-done(((f32[16,4096]{1,0:T(8,128)}), f32[16,4096]{1,0:T(8,128)}) %all-reduce.3.cloned.1.call-update) | async-done | bytes 262160 | tf_op jit(solution)/shard_map/psum | solution.py:110
  489.7 10.4 %all-to-all-start.2 = ((f32[8,64,128]{2,0,1:T(8,128)}), f32[8,64,128]{2,0,1:T(8,128)S(1)}, u32[]{:S(2)}, u32[]{:S(2)}) async-start(f32[8,64,128]{2,0,1:T(8,128)} %copy.26), calls=%async_computation.2 | async-start | bytes 524288 | tf_op jit(solution)/shard_map/all_to_all | solution.py:191
  500.3 10.7 %all-to-all-done.2 = f32[8,64,128]{2,0,1:T(8,128)S(1)} async-done(((f32[8,64,128]{2,0,1:T(8,128)}), f32[8,64,128]{2,0,1:T(8,128)S(1)}, u32[]{:S(2)}, u32[]{:S(2)}) %all-to-all-start.2) | async-done | bytes 262176 | tf_op jit(solution)/shard_map/all_to_all | solution.py:191
  512.1 6.9 %collective-permute-start.1 = (f32[8,128]{1,0:T(8,128)S(1)}, f32[8,128]{1,0:T(8,128)S(1)}, u32[]{:S(2)}, u32[]{:S(2)}) collective-permute-start(f32[8,128]{1,0:T(8,128)S(1)} %get-tuple-element.394), channel_id=1, source_target_pairs={{2,0},{4,2},{6,4},{8,6},{10,8},{12,10},{14,12},{16,14},{18,16},{20... | collective-permute-start | bytes 12296 | tf_op jit(solution)/shard_map/ppermute | solution.py:20
  519.0 1.6 collective-permute-done
  520.8 20.1 %fusion.46 = f32[8,8192]{1,0:T(8,128)} fusion(f32[64,128]{1,0:T(8,128)S(1)} %bitcast.965, s32[64,128]{1,0:T(8,128)S(1)} %get-tuple-element.417, f32[64,128]{1,0:T(8,128)S(1)} %bitcast.966, s32[64,128]{1,0:T(8,128)S(1)} %get-tuple-element.416, f32[64,128]{1,0:T(8,128)S(1)} %bitcast.967, s32[64,128]{1,0:T(8,128)S(1)} %get-tuple-element.415, ...), kind=kOutput, calls=%fused_computation.298 | convolution fusion | flops 364904448 | bytes 1507328 | tf_op jit(solution)/shard_map/rnw,nwk->rnk/dot_general | solution.py:134
  (285 shorter events, 46.7 us)
Async XLA Ops:
  11.4 370.0 %all-to-all-start.1 = ((bf16[3,1,64,128]{3,0,1,2:T(4,128)(2,1)}), bf16[3,1,64,128]{3,0,1,2:T(4,128)(2,1)S(1)}, u32[]{:S(2)}, u32[]{:S(2)}) async-start(bf16[3,1,64,128]{3,0,1,2:T(4,128)(2,1)} %copy.24), calls=%async_computation.1 | async-start | bytes 131072 | tf_op jit(solution)/shard_map/all_to_all | solution.py:170
  379.1 2.2 copy-start.1
  381.3 21.9 %all-to-all-start = ((bf16[6,16,64,128]{3,1,0,2:T(8,128)(2,1)}), bf16[6,16,64,128]{3,1,0,2:T(8,128)(2,1)S(1)}, u32[]{:S(2)}, u32[]{:S(2)}) async-start(bf16[6,16,64,128]{3,1,0,2:T(8,128)(2,1)} %copy.22), calls=%async_computation | async-start | bytes 3145728 | tf_op jit(solution)/shard_map/all_to_all | solution.py:169
  386.0 101.6 %all-reduce.3.cloned.1.call-start = ((), (), s32[]{:S(2)}) async-start(), calls=%async_computation.3 | async-start | bytes 524288 | tf_op jit(solution)/shard_map/psum | solution.py:110
  386.3 17.9 %copy-start = (f32[56]{0:T(128)S(1)}, f32[56]{0:T(128)}, u32[]{:S(2)}) copy-start(f32[56]{0:T(128)} %param.17) | copy-start | bytes 676
  386.4 17.9 %copy-start.4 = (f32[3,56]{1,0:T(4,128)S(1)}, f32[3,56]{1,0:T(4,128)}, u32[]{:S(2)}) copy-start(f32[3,56]{1,0:T(4,128)} %param.16) | copy-start | bytes 2020
  404.2 63.8 %copy-start.3 = (s32[7,8192]{1,0:T(8,128)S(1)}, s32[7,8192]{1,0:T(8,128)}, u32[]{:S(2)}) copy-start(s32[7,8192]{1,0:T(8,128)} %param.14) | copy-start | bytes 688132
  467.3 0.7 copy-start.2
  489.7 21.2 %all-to-all-start.2 = ((f32[8,64,128]{2,0,1:T(8,128)}), f32[8,64,128]{2,0,1:T(8,128)S(1)}, u32[]{:S(2)}, u32[]{:S(2)}) async-start(f32[8,64,128]{2,0,1:T(8,128)} %copy.26), calls=%async_computation.2 | async-start | bytes 524288 | tf_op jit(solution)/shard_map/all_to_all | solution.py:191
  511.4 9.1 %collective-permute-start = (f32[8,128]{1,0:T(8,128)S(1)}, f32[8,128]{1,0:T(8,128)S(1)}, u32[]{:S(2)}, u32[]{:S(2)}) collective-permute-start(f32[8,128]{1,0:T(8,128)S(1)} %get-tuple-element.393), channel_id=1, source_target_pairs={{0,2},{2,4},{4,6},{6,8},{8,10},{10,12},{12,14},{14,16},{16,18},{18... | collective-permute-start | bytes 12296 | tf_op jit(solution)/shard_map/ppermute | solution.py:17
  512.1 8.5 %collective-permute-start.1 = (f32[8,128]{1,0:T(8,128)S(1)}, f32[8,128]{1,0:T(8,128)S(1)}, u32[]{:S(2)}, u32[]{:S(2)}) collective-permute-start(f32[8,128]{1,0:T(8,128)S(1)} %get-tuple-element.394), channel_id=1, source_target_pairs={{2,0},{4,2},{6,4},{8,6},{10,8},{12,10},{14,12},{16,14},{18,16},{20... | collective-permute-start | bytes 12296 | tf_op jit(solution)/shard_map/ppermute | solution.py:20
Sparse Core Ops, SparseCore 0:
  468.2 19.3 all-reduce.2
where the time goes:
time: 553 us; the launch traced here: 548 us
  blocking collectives  349 us (63%)
  other arithmetic  64.2 us (12%)
  waiting for transfers between devices  48.5 us (9%)
  starting transfers between devices  34.2 us (6%)
  matrix products  22.3 us (4%)
  between operations  14.6 us (3%)
  local copies, waits for them, and re-layouts  12.6 us (2%)
    unnamed x1, blocking collectives  349 us
    reduce_sum x56, other arithmetic, column_heat(): jnp.sum(absorbed[layer_index] * (diffuse + direct[layer_index]), axis=0)  55.5 us
    dot_general x1, matrix products, interpolate(): jnp.einsum('rnw,nwk->rnk', windows, mixing, preferred_element_type=jnp.fl...  20.1 us
    psum x1, waiting for transfers between devices, reduce_bands(): summed = lax.psum(heating, 'gpt')  19.4 us
    all_to_all x1, waiting for transfers between devices, local(): lax.all_to_all(send_fields, 'cell', split_axis=2, concat_axis=2, tiled=True)  16.9 us
    all_to_all x1, starting transfers between devices, local(): lax.all_to_all(send_geometry, 'cell', split_axis=2, concat_axis=2, tiled=...  11.5 us
  transfers between devices with their start and end apart: 6, of which 4 were waited for; matrix products, arithmetic and copies ran while one was open for 2% of the time, Pallas kernels for 0%

commit v1 on v0

--- a/solution.py
+++ b/solution.py
@@ -107,7 +107,8 @@
 
 
 def reduce_bands(heating):
-    summed = lax.psum(heating, "gpt")
+    keys_push = lambda block_here: jnp.sum(lax.all_gather(block_here, "gpt"), axis=0)
+    summed = keys_push(heating)
     each_rows = heating.shape[0] // lax.axis_size("gpt")
     return lax.dynamic_slice_in_dim(summed, lax.axis_index("gpt") * each_rows, each_rows, 0)
 

time: 553 us -> 516 us (0.933)
  waiting for transfers between devices: 48.5 us -> 29.2 us
  between operations: 14.6 us -> 1.18 us
  starting transfers between devices: 34.2 us -> 28.5 us
    psum x1 -> x0, waiting for transfers between devices: 19.4 us -> none  [reduce_bands(): summed = lax.psum(heating, 'gpt')]
    all_to_all x1, starting transfers between devices: 10.4 us -> 4.63 us  [local(): lax.all_to_all(returned, 'cell', split_axis=1, concat_axis=1, tiled=True)]
  transfers between devices with their start and end apart: 6 -> 5, of which waited for: 4 -> 3; matrix products, arithmetic and copies ran while one was open for 2% -> 2% of each run, Pallas kernels for 0% -> 0%
where the time goes in v1:
time: 516 us; the launch traced here: 510 us
  blocking collectives  352 us (68%)
  other arithmetic  64.2 us (12%)
  waiting for transfers between devices  29.2 us (6%)
  starting transfers between devices  28.5 us (6%)
  matrix products  22.3 us (4%)
  local copies, waits for them, and re-layouts  11.3 us (2%)
    unnamed x1, blocking collectives  349 us
    reduce_sum x56, other arithmetic, column_heat(): jnp.sum(absorbed[layer_index] * (diffuse + direct[layer_index]), axis=0)  55.5 us
    dot_general x1, matrix products, interpolate(): jnp.einsum('rnw,nwk->rnk', windows, mixing, preferred_element_type=jnp.fl...  20.1 us
    all_to_all x1, waiting for transfers between devices, local(): lax.all_to_all(send_fields, 'cell', split_axis=2, concat_axis=2, tiled=True)  16.8 us
    all_to_all x1, starting transfers between devices, local(): lax.all_to_all(send_geometry, 'cell', split_axis=2, concat_axis=2, tiled=...  11.5 us
    all_to_all x1, waiting for transfers between devices, local(): lax.all_to_all(returned, 'cell', split_axis=1, concat_axis=1, tiled=True)  10.8 us
  transfers between devices with their start and end apart: 5, of which 3 were waited for; matrix products, arithmetic and copies ran while one was open for 2% of the time, Pallas kernels for 0%

profile of v1, /device:TPU:0, one launch (start us, length us, event | category | flops | bytes accessed | tf_op | source)
XLA Modules:
  0.0 510.4 jit_solution(15732824629089534210)
XLA Ops:
  4.8 11.5 %all-to-all-start.1 = ((bf16[3,1,64,128]{3,0,1,2:T(4,128)(2,1)}), bf16[3,1,64,128]{3,0,1,2:T(4,128)(2,1)S(1)}, u32[]{:S(2)}, u32[]{:S(2)}) async-start(bf16[3,1,64,128]{3,0,1,2:T(4,128)(2,1)} %copy.24), calls=%async_computation.1 | async-start | bytes 131072 | tf_op jit(solution)/shard_map/all_to_all | solution.py:171
  16.4 1.3 dynamic-slice
  19.3 349.4 %all-reduce = s32[4096]{0:T(1024)S(1)} all-reduce(s32[4096]{0:T(1024)S(1)} %dynamic-update-slice), channel_id=1, replica_groups=mesh['cell'=64,'gpt'=2] {'cell'}, use_global_device_ids=true, to_apply=%add | all-reduce | flops 4096 | bytes 32768
  370.0 1.8 copy.31
  373.0 2.2 copy.22
  375.2 4.8 all-to-all-start
  380.4 16.8 %all-to-all-done = bf16[6,16,64,128]{3,1,0,2:T(8,128)(2,1)S(1)} async-done(((bf16[6,16,64,128]{3,1,0,2:T(8,128)(2,1)}), bf16[6,16,64,128]{3,1,0,2:T(8,128)(2,1)S(1)}, u32[]{:S(2)}, u32[]{:S(2)}) %all-to-all-start) | async-done | bytes 1572896 | tf_op jit(solution)/shard_map/all_to_all | solution.py:170
  398.2 63.0 %while.13 = (s32[]{:T(128)}, f32[16,4096]{1,0:T(8,128)S(1)}, f32[3,56]{1,0:T(4,128)S(1)}, bf16[6,16,4096]{2,1,0:T(8,128)(2,1)S(1)}, f32[56]{0:T(128)S(1)}, /*ind...) while((s32[]{:T(128)}, f32[16,4096]{1,0:T(8,128)S(1)}, ...), condition=%wide.region_23.24_spmd, body=%wide.region_6.23_spmd.sunk | while | flops 70601744 | bytes 23048272 | solution.py:88
  399.8 5.0 multiply_reduce_fusion.30
  409.2 1.3 multiply_reduce_fusion.40
  410.5 1.3 multiply_reduce_fusion.36
  415.4 5.0 multiply_reduce_fusion.30
  424.8 1.3 multiply_reduce_fusion.40
  426.1 1.3 multiply_reduce_fusion.36
  431.0 5.0 multiply_reduce_fusion.30
  441.7 1.3 multiply_reduce_fusion.36
  446.6 5.0 multiply_reduce_fusion.30
  457.3 1.3 multiply_reduce_fusion.36
  461.3 2.2 all-gather
  464.7 4.6 all-to-all-start.2
  469.5 10.8 %all-to-all-done.2 = f32[8,64,128]{2,0,1:T(8,128)S(1)} async-done(((f32[8,64,128]{2,0,1:T(8,128)}), f32[8,64,128]{2,0,1:T(8,128)S(1)}, u32[]{:S(2)}, u32[]{:S(2)}) %all-to-all-start.2) | async-done | bytes 262176 | tf_op jit(solution)/shard_map/all_to_all | solution.py:192
  481.5 6.9 %collective-permute-start.1 = (f32[8,128]{1,0:T(8,128)S(1)}, f32[8,128]{1,0:T(8,128)S(1)}, u32[]{:S(2)}, u32[]{:S(2)}) collective-permute-start(f32[8,128]{1,0:T(8,128)S(1)} %get-tuple-element.394), channel_id=1, source_target_pairs={{2,0},{4,2},{6,4},{8,6},{10,8},{12,10},{14,12},{16,14},{18,16},{20... | collective-permute-start | bytes 12296 | tf_op jit(solution)/shard_map/ppermute | solution.py:20
  488.4 1.6 collective-permute-done
  490.1 20.1 %fusion.46 = f32[8,8192]{1,0:T(8,128)} fusion(f32[64,128]{1,0:T(8,128)S(1)} %bitcast.967, s32[64,128]{1,0:T(8,128)S(1)} %get-tuple-element.417, f32[64,128]{1,0:T(8,128)S(1)} %bitcast.968, s32[64,128]{1,0:T(8,128)S(1)} %get-tuple-element.416, f32[64,128]{1,0:T(8,128)S(1)} %bitcast.969, s32[64,128]{1,0:T(8,128)S(1)} %get-tuple-element.415, ...), kind=kOutput, calls=%fused_computation.298 | convolution fusion | flops 364904448 | bytes 1507328 | tf_op jit(solution)/shard_map/rnw,nwk->rnk/dot_general | solution.py:135
  (282 shorter events, 45.4 us)
Async XLA Ops:
  4.8 370.4 %all-to-all-start.1 = ((bf16[3,1,64,128]{3,0,1,2:T(4,128)(2,1)}), bf16[3,1,64,128]{3,0,1,2:T(4,128)(2,1)S(1)}, u32[]{:S(2)}, u32[]{:S(2)}) async-start(bf16[3,1,64,128]{3,0,1,2:T(4,128)(2,1)} %copy.24), calls=%async_computation.1 | async-start | bytes 131072 | tf_op jit(solution)/shard_map/all_to_all | solution.py:171
  371.8 1.0 copy-start.1
  375.2 4.8 copy-start.2
  375.2 22.0 %all-to-all-start = ((bf16[6,16,64,128]{3,1,0,2:T(8,128)(2,1)}), bf16[6,16,64,128]{3,1,0,2:T(8,128)(2,1)S(1)}, u32[]{:S(2)}, u32[]{:S(2)}) async-start(bf16[6,16,64,128]{3,1,0,2:T(8,128)(2,1)} %copy.22), calls=%async_computation | async-start | bytes 3145728 | tf_op jit(solution)/shard_map/all_to_all | solution.py:170
  380.4 17.8 %copy-start = (f32[56]{0:T(128)S(1)}, f32[56]{0:T(128)}, u32[]{:S(2)}) copy-start(f32[56]{0:T(128)} %param.17) | copy-start | bytes 676
  380.4 17.8 %copy-start.3 = (f32[3,56]{1,0:T(4,128)S(1)}, f32[3,56]{1,0:T(4,128)}, u32[]{:S(2)}) copy-start(f32[3,56]{1,0:T(4,128)} %param.16) | copy-start | bytes 2020
  464.7 15.6 %all-to-all-start.2 = ((f32[8,64,128]{2,0,1:T(8,128)}), f32[8,64,128]{2,0,1:T(8,128)S(1)}, u32[]{:S(2)}, u32[]{:S(2)}) async-start(f32[8,64,128]{2,0,1:T(8,128)} %copy.26), calls=%async_computation.2 | async-start | bytes 524288 | tf_op jit(solution)/shard_map/all_to_all | solution.py:192
  480.8 9.1 %collective-permute-start = (f32[8,128]{1,0:T(8,128)S(1)}, f32[8,128]{1,0:T(8,128)S(1)}, u32[]{:S(2)}, u32[]{:S(2)}) collective-permute-start(f32[8,128]{1,0:T(8,128)S(1)} %get-tuple-element.393), channel_id=1, source_target_pairs={{0,2},{2,4},{4,6},{6,8},{8,10},{10,12},{12,14},{14,16},{16,18},{18... | collective-permute-start | bytes 12296 | tf_op jit(solution)/shard_map/ppermute | solution.py:17
  481.5 8.5 %collective-permute-start.1 = (f32[8,128]{1,0:T(8,128)S(1)}, f32[8,128]{1,0:T(8,128)S(1)}, u32[]{:S(2)}, u32[]{:S(2)}) collective-permute-start(f32[8,128]{1,0:T(8,128)S(1)} %get-tuple-element.394), channel_id=1, source_target_pairs={{2,0},{4,2},{6,4},{8,6},{10,8},{12,10},{14,12},{16,14},{18,16},{20... | collective-permute-start | bytes 12296 | tf_op jit(solution)/shard_map/ppermute | solution.py:20
